TPU v7x, 32 devices: a whole 2x2x4 slice. The times are simulated.
32 devices in a mesh: strings: 2 (over y), ka: 4 (over x, core), coef: 4 (over z).
Axes of the slice: x: 2, y: 2, z: 4, core: 2. Of those that a mesh axis runs over, the one named last changes fastest.
Arguments:
- wavefunctions: float32 [8, 49152, 384], P(('strings', 'ka'), 'coef'), parts along dimension 0, may hold values from -8 to 8
Outputs:
- transported: float32 [8, 49152, 384], P(('strings', 'ka'), 'coef'), parts along dimension 0
There are 2 independent parts, one for each index of `strings`. A program takes and returns all parts, laid end to end along the dimension named above; each array names one. Nothing has to cross between parts.
All inputs are finite; a program needn't handle non-finite values.
Results may differ from a plain program's by a relative error of at most 0.0003.
Values sent between devices are 32-bit elements; how exact they have to be, the bound alone decides.
No kernel may reach another device: no remote copies, remote signals or barrier semaphores. Data moves between devices by JAX's collectives and lax.ppermute only.
A program may use at most 128 MiB of HBM per device.

v0:
```python
import functools
import math

import jax
import jax.numpy as jnp
from jax import lax
from jax.experimental import pallas as pl
from jax.experimental.pallas import tpu as pltpu
from jax.sharding import PartitionSpec as P


NS_ITERS = 3
F32 = jnp.float32
BF16 = jnp.bfloat16


def split(x):
    high = x.astype(BF16)
    return high, (x - high.astype(F32)).astype(BF16)


def dot(a, b):
    return lax.dot_general(a, b, (((1,), (0,)), ((), ())), preferred_element_type=F32)


def product3(a, b):
    size = b[0].shape[1]
    wide = dot(a[0], jnp.concatenate(b, axis=1))
    return wide[:, :size] + (wide[:, size:] + dot(a[1], b[0]))


def polar(matrix, total):
    size = matrix.shape[0]
    margin = matrix * (1.0 / total)
    scale = jnp.sqrt(size * (jnp.sum(margin * margin) / (size * size)) + 1e-06)
    iterate = margin / scale
    for _ in range(NS_ITERS):
        parts = split(iterate)
        gram = product3(split(iterate.T), parts)
        iterate = 1.5 * iterate - 0.5 * product3(parts, split(gram))
    return iterate


def polar_kernel(total, sum_ref, *refs):
    refs[-1][...] = polar(sum_ref[...], total)


VMEM = pl.BlockSpec(memory_space=pltpu.VMEM)
HBM = pl.BlockSpec(memory_space=pltpu.HBM)
ANY = pl.BlockSpec(memory_space=pl.ANY)


def polar_call(matrix, total, behind):
    return pl.pallas_call(
        functools.partial(polar_kernel, total),
        out_shape=jax.ShapeDtypeStruct(matrix.shape, F32),
        in_specs=[VMEM, ANY],
        out_specs=VMEM,
        name="polar",
    )(matrix, behind)


def rotate_kernel(total, rows_ref, turned_ref, later_ref, wave, out, wave_buf, out_buf, near_ref, rest_ref, low_ref, in_sem, out_sem):
    size = wave_buf.shape[1]
    block = out_buf.shape[1]
    steps = wave_buf.shape[0] // block
    main = size // 256 * 256
    rest = size - main

    def fetch(c):
        piece = pl.ds(pl.multiple_of(c * block, block), block)
        return pltpu.make_async_copy(wave.at[piece], wave_buf.at[piece], in_sem.at[c])

    def put(c):
        piece = pl.ds(pl.multiple_of(c * block, block), block)
        return pltpu.make_async_copy(out_buf.at[c % 2], out.at[piece], out_sem.at[c % 2])

    for c in range(steps):
        fetch(c).start()
    closing = polar(rows_ref[...] + turned_ref[...].T, total)
    high, low = split(product3(split(later_ref[...].T), split(closing.T)))
    near_ref[0:size] = high[:, :main]
    near_ref[size:] = high[:, :main]
    rest_ref[0:size, :rest] = high[:, main:]
    rest_ref[size:, :rest] = high[:, main:]
    rest_ref[0:size, rest:] = low[:, main:]
    rest_ref[size:, rest:] = jnp.zeros((size, rest), BF16)
    low_ref[...] = low[:, :main]

    def body(c, _):
        fetch(c).wait()

        @pl.when(c >= 2)
        def _():
            put(c - 2).wait()

        high, low = split(wave_buf[pl.ds(pl.multiple_of(c * block, block), block)])
        both = jnp.concatenate([high, low], axis=1)
        out_buf[c % 2, :, :main] = dot(both, near_ref[...]) + dot(high, low_ref[...])
        wide = dot(both, rest_ref[...])
        out_buf[c % 2, :, main:] = wide[:, :rest] + wide[:, rest:]
        put(c).start()
        return 0

    lax.fori_loop(0, steps, body, 0)
    for c in range(max(steps - 2, 0), steps):
        put(c).wait()


def rotate_call(rows, turned, later, wave, total):
    count, size = wave.shape
    block = 1024
    while count % block:
        block //= 2
    main = size // 256 * 256
    rest = size - main
    hbm = pl.BlockSpec(memory_space=pltpu.HBM)
    return pl.pallas_call(
        functools.partial(rotate_kernel, total),
        out_shape=jax.ShapeDtypeStruct(wave.shape, F32),
        in_specs=[VMEM, VMEM, VMEM, hbm],
        out_specs=hbm,
        scratch_shapes=[
            pltpu.VMEM((count, size), F32),
            pltpu.VMEM((2, block, size), F32),
            pltpu.VMEM((2 * size, main), BF16),
            pltpu.VMEM((2 * size, 2 * rest), BF16),
            pltpu.VMEM((size, main), BF16),
            pltpu.SemaphoreType.DMA((count // block,)),
            pltpu.SemaphoreType.DMA((2,)),
        ],
        name="rotate",
    )(rows, turned, later, wave)


def few(axis):
    return lax.axis_size(axis) in (2, 4)


def xor_permute(x, distance, ends_only=False):
    points, count = lax.axis_size("ka"), lax.axis_size("coef")
    some = (0, points - 1) if ends_only else range(points)
    route = [(k * count + i, k * count + (i ^ distance)) for k in some for i in range(count)]
    return lax.ppermute(x, ("ka", "coef"), route)


def scatter_sum(x, ends_only=False):
    count = lax.axis_size("coef")
    if not few("coef"):
        return lax.psum_scatter(x, "coef", scatter_dimension=0, tiled=True)
    share = x.shape[0] // count
    me = lax.axis_index("coef")
    total = lax.dynamic_slice_in_dim(x, me * share, share, 0)
    parts = [
        xor_permute(lax.dynamic_slice_in_dim(x, (me ^ d) * share, share, 0), d, ends_only)
        for d in range(count - 1, 0, -1)
    ]
    for part in parts:
        total = total + part
    return total


def gather_rows(x, ends_only=False):
    count = lax.axis_size("coef")
    if not few("coef"):
        return lax.all_gather(x, "coef", axis=0, tiled=True)
    me = lax.axis_index("coef")
    pieces = jnp.stack([x] + [xor_permute(x, d, ends_only) for d in range(1, count)])
    return jnp.concatenate(
        [lax.dynamic_index_in_dim(pieces, me ^ j, 0, keepdims=False) for j in range(count)]
    )


def end_sum(x, distance=1):
    count = lax.axis_size("coef")
    if not few("coef"):
        return lax.psum(x, "coef")
    while distance < count:
        x = x + xor_permute(x, distance, True)
        distance *= 2
    return x


def ends(x):
    count = lax.axis_size("ka")
    if count != 4:
        both = lax.all_gather(x, "ka", axis=0)
        return both[0], both[count - 1]
    me = lax.axis_index("ka")
    across = lax.ppermute(x, "ka", [(0, 2), (3, 1)])
    own = jnp.where((me == 0) | (me == 3), x, across)
    other = lax.ppermute(own, "ka", [(0, 1), (1, 0), (2, 3), (3, 2)])
    even = (me == 0) | (me == 2)
    return jnp.where(even, own, other), jnp.where(even, other, own)


def copy_rows_kernel(pieces, wave, *refs):
    outs = refs[: len(pieces)]
    bufs = refs[len(pieces) : 2 * len(pieces)]
    in_sem, out_sem = refs[2 * len(pieces) :]
    ins = [
        pltpu.make_async_copy(wave.at[pl.ds(low, high - low)], buf, in_sem.at[i])
        for i, ((low, high), buf) in enumerate(zip(pieces, bufs))
    ]
    puts = [pltpu.make_async_copy(buf, out, out_sem.at[i]) for i, (buf, out) in enumerate(zip(bufs, outs))]
    for copy in ins:
        copy.start()
    for get, put in zip(ins, puts):
        get.wait()
        put.start()
    for put in puts:
        put.wait()


def copy_rows(wave, pieces):
    size = wave.shape[1]
    shapes = [(high - low, size) for low, high in pieces]
    return pl.pallas_call(
        functools.partial(copy_rows_kernel, pieces),
        out_shape=[jax.ShapeDtypeStruct(s, F32) for s in shapes],
        in_specs=[HBM],
        out_specs=[HBM] * len(pieces),
        scratch_shapes=[pltpu.VMEM(s, F32) for s in shapes]
        + [pltpu.SemaphoreType.DMA((len(pieces),)), pltpu.SemaphoreType.DMA((len(pieces),))],
        name="copy_rows",
    )(wave)


def cuts(unit, shares):
    bounds = [0]
    for share in shares:
        bounds.append(bounds[-1] + share * unit)
    return list(zip(bounds[:-1], bounds[1:]))


def meet_kernel(flag, at_ref, left_ref, right_ref, total_ref, *refs):
    out_ref = refs[-1]

    @pl.when(pl.program_id(0) == 0)
    def _():
        out_ref[...] = total_ref[...]

    @pl.when(at_ref[flag] == 1)
    def _():
        left, right = split(left_ref[...]), split(right_ref[...])
        dims = (((0,), (0,)), ((), ()))
        size = right_ref.shape[1]
        both = lax.dot_general(left[0], jnp.concatenate(right, axis=1), dims, preferred_element_type=F32)
        rest = lax.dot_general(left[1], right[0], dims, preferred_element_type=F32)
        out_ref[...] += both[:, :size] + (both[:, size:] + rest)


def meet(left, left_at, right, right_at, rows, total, at, flag, behind=()):
    lanes, size = left.shape[1], right.shape[1]
    block = math.gcd(rows, left_at, right_at)
    while block > 1024:
        block //= 2 if block % 2 == 0 else 3
    left_at, right_at = left_at // block, right_at // block

    def left_map(i, at):
        return ((left_at + i) * at[flag], 0)

    def right_map(i, at):
        further = at[0] // block if flag == 3 else 0
        return ((right_at + further + i) * at[flag], 0)

    whole = pl.BlockSpec(total.shape, lambda i, at: (0, 0))
    return pl.pallas_call(
        functools.partial(meet_kernel, flag),
        out_shape=jax.ShapeDtypeStruct(total.shape, F32),
        grid_spec=pltpu.PrefetchScalarGridSpec(
            num_scalar_prefetch=1,
            grid=(rows // block,),
            in_specs=[
                pl.BlockSpec((block, lanes), left_map),
                pl.BlockSpec((block, size), right_map),
                whole,
            ]
            + [ANY] * len(behind),
            out_specs=whole,
        ),
        cost_estimate=pl.CostEstimate(
            flops=6 * rows * lanes * size, bytes_accessed=4 * rows * (lanes + size), transcendentals=0
        ),
        name="meet",
    )(at, left, right, total, *behind)


def cut_kernel(pieces, start, wave, *refs):
    outs = refs[: len(pieces)]
    buf, in_sem, out_sem = refs[len(pieces) :]
    half, _ = buf.shape
    begin = pl.multiple_of(start[0], 8)
    share = half // in_sem.shape[0]
    gets = [
        pltpu.make_async_copy(
            wave.at[pl.ds(begin + i * share, share)], buf.at[pl.ds(i * share, share)], in_sem.at[i]
        )
        for i in range(in_sem.shape[0])
    ]
    puts = [
        pltpu.make_async_copy(
            buf.at[pl.ds(low, high - low), pl.ds(left, right - left)], out, out_sem.at[i]
        )
        for i, (((low, high), (left, right)), out) in enumerate(zip(pieces, outs))
    ]
    for get in gets:
        get.start()
    landed = 0
    for ((low, high), _), put in zip(pieces, puts):
        while landed * share < high:
            gets[landed].wait()
            landed += 1
        put.start()
    for get in gets[landed:]:
        get.wait()
    for put in puts:
        put.wait()


def cut_call(wave, start, half, pieces):
    shapes = [(high - low, right - left) for (low, high), (left, right) in pieces]
    return pl.pallas_call(
        functools.partial(cut_kernel, pieces),
        out_shape=[jax.ShapeDtypeStruct(s, F32) for s in shapes],
        in_specs=[pl.BlockSpec(memory_space=pltpu.SMEM), HBM],
        out_specs=[HBM] * len(shapes),
        scratch_shapes=[
            pltpu.VMEM((half, wave.shape[1]), F32),
            pltpu.SemaphoreType.DMA((6,)),
            pltpu.SemaphoreType.DMA((len(shapes),)),
        ],
        name="cut",
    )(jnp.reshape(start, (1,)).astype(jnp.int32), wave)


FIRSTS = (3, 5, 3, 1)
WIDES = (6, 6)
LATES = (6, 4, 2)


def whole_step(wavefunctions):
    wave = wavefunctions[0]
    count, size = wave.shape
    points = lax.axis_size("ka")
    position = lax.axis_index("ka")
    coefs = lax.axis_size("coef")
    total = count * coefs
    half = count // 2
    unit = half // 12
    wide = size - 128
    forward = [(k, k + 1) for k in range(points - 1)]
    backward = [(k + 1, k) for k in range(points - 1)]
    closing = [(0, points - 1), (points - 1, 0)]
    streamed = []
    start = jnp.where(position == 0, 0, half)
    at_end = (position == 0) | (position == points - 1)
    at = jnp.stack([half - start, position > 0, position < points - 1, at_end]).astype(jnp.int32)

    def stream(*pieces):
        streamed.append(tuple(lax.ppermute(x, "ka", way) for x, way in pieces))

    firsts = cuts(unit, FIRSTS)
    for low, high in firsts:
        up, down = copy_rows(wave, [(low, high), (half + low, half + high)])
        stream((up, forward), (down, backward))

    wides, lates = cuts(unit, WIDES), cuts(unit, LATES)
    blocks = [(rows, (0, wide)) for rows in wides] + [(rows, (wide, size)) for rows in lates]
    up, down = streamed[-2]
    token = lax.ppermute(up[:8, :128] + down[:8, :128], "ka", [(k, k ^ 1) for k in range(points)])
    blocks = cut_call(wave, start, half, blocks)
    for block in blocks:
        stream((block, closing))

    def close(i, rows, block, *behind):
        low, high = rows
        return meet(streamed[i][0], 0, wave, low, high - low, block, at, 3, behind)

    at_later = at_earlier = jnp.zeros((size, size), F32)
    for i, (low, high) in enumerate(firsts):
        up, down = streamed[i]
        at_later = meet(up, 0, wave, low, high - low, at_later, at, 1)
        at_earlier = meet(wave, half + low, down, 0, high - low, at_earlier, at, 2)

    both = jnp.stack([at_later, at_earlier])
    share = size // coefs
    both = scatter_sum(both.reshape(2, coefs, share, size).transpose(1, 0, 2, 3).reshape(2 * size, size))
    margin_share = both[:share] + lax.ppermute(both[share:], "ka", forward)
    early = jnp.zeros((wide, size), F32)
    first = len(firsts)
    early = close(first, wides[0], early, token)
    early = close(first + 1, wides[1], early)
    unitary = polar_call(gather_rows(margin_share), total, early)

    mine = lax.axis_index("coef")
    share = size // coefs
    own = jnp.where(position == 0, jnp.eye(size, dtype=F32), unitary)
    product = lax.dynamic_slice_in_dim(own, mine * share, share, 0)
    for k in range(1, points - 1):
        came = lax.ppermute(product, "ka", [(k, k + 1)])
        longer = lax.dot_general(came, own, (((1,), (0,)), ((), ())), precision=lax.Precision.HIGH)
        product = jnp.where(position == k + 1, longer, product)
    later = gather_rows(product)

    pair = early + xor_permute(early, 1, True) if few("coef") else early
    late = close(first + 2, lates[0], jnp.zeros((128, size), F32), product, pair)
    early = ends(end_sum(pair, 2) if few("coef") else end_sum(early))
    late = close(first + 3, lates[1], late, *early)
    late = close(first + 4, lates[2], late)
    late = ends(end_sum(late))
    rows, turned = [jnp.concatenate(pair) for pair in zip(early, late)]
    return rotate_call(rows, turned, later, wave, total)[None]


def solution(mesh):
    spec = P(("strings", "ka"), "coef", None)
    return jax.shard_map(whole_step, mesh=mesh, in_specs=(spec,), out_specs=spec, check_vma=False)
```

profile of v0, /device:TPU:7, one launch (start us, length us, event | category | flops | bytes accessed | tf_op | source)
XLA Modules:
  0.0 370.7 jit_solution(17546639740918717376)
XLA Ops:
  0.0 3.8 %copy_rows.7 = (f32[1536,384]{1,0:T(8,128)}, f32[1536,384]{1,0:T(8,128)}) custom-call(f32[12288,384]{1,0:T(8,128)} %bitcast.40), custom_call_target="tpu_custom_call" | custom-call | tf_op jit(solution)/shard_map/copy_rows/pallas_call | solution.py:218
  5.1 4.7 %collective-permute-start.17 = (f32[1536,384]{1,0:T(8,128)}, f32[1536,384]{1,0:T(8,128)}, u32[]{:S(2)}, u32[]{:S(2)}) collective-permute-start(f32[1536,384]{1,0:T(8,128)} %get-tuple-element.30), channel_id=1, source_target_pairs={{4,0},{8,4},{12,8},{5,1},{9,5},{13,9},{6,2},{10,6},{14,10},{7,3},{... | collective-permute-start | bytes 7077896 | tf_op jit(solution)/shard_map/ppermute | solution.py:361
  9.8 3.9 %copy_rows.4 = (f32[1536,384]{1,0:T(8,128)}, f32[1536,384]{1,0:T(8,128)}) custom-call(f32[12288,384]{1,0:T(8,128)} %bitcast.41), custom_call_target="tpu_custom_call" | custom-call | tf_op jit(solution)/shard_map/copy_rows/pallas_call | solution.py:218
  15.0 5.7 %copy_rows.6 = (f32[2560,384]{1,0:T(8,128)}, f32[2560,384]{1,0:T(8,128)}) custom-call(f32[12288,384]{1,0:T(8,128)} %bitcast.42), custom_call_target="tpu_custom_call" | custom-call | tf_op jit(solution)/shard_map/copy_rows/pallas_call | solution.py:218
  21.9 5.6 %collective-permute-start.16 = (f32[2560,384]{1,0:T(8,128)}, f32[2560,384]{1,0:T(8,128)}, u32[]{:S(2)}, u32[]{:S(2)}) collective-permute-start(f32[2560,384]{1,0:T(8,128)} %get-tuple-element.29), channel_id=1, source_target_pairs={{4,0},{8,4},{12,8},{5,1},{9,5},{13,9},{6,2},{10,6},{14,10},{7,3},{... | collective-permute-start | bytes 11796488 | tf_op jit(solution)/shard_map/ppermute | solution.py:361
  27.5 10.8 %collective-permute-start.3 = (f32[1536,384]{1,0:T(8,128)}, f32[1536,384]{1,0:T(8,128)}, u32[]{:S(2)}, u32[]{:S(2)}) collective-permute-start(f32[1536,384]{1,0:T(8,128)} %get-tuple-element.21), channel_id=1, source_target_pairs={{4,0},{8,4},{12,8},{5,1},{9,5},{13,9},{6,2},{10,6},{14,10},{7,3},{... | collective-permute-start | bytes 7077896 | tf_op jit(solution)/shard_map/ppermute | solution.py:361
  38.4 7.4 %cut.1 = (f32[3072,256]{1,0:T(8,128)}, f32[3072,256]{1,0:T(8,128)}, f32[3072,128]{1,0:T(8,128)}, f32[2048,128]{1,0:T(8,128)}, f32[1024,128]{1,0:T(8,128)}) custom-call(s32[1]{0:T(128)} %bitcast.4.start, f32[12288,384]{1,0:T(8,128)} %bitcast.43), custom_call_target="tpu_custom_call" | custom-call | tf_op jit(solution)/shard_map/cut/pallas_call | solution.py:323
  45.8 1.9 collective-permute-start.1
  47.7 3.6 collective-permute-start
  51.4 2.3 copy_rows.5
  56.6 5.3 %meet.15.total_ref = f32[384,384]{1,0:T(8,128)} custom-call(s32[4]{0:T(128)} %pad_add_fusion.at_ref, f32[1536,384]{1,0:T(8,128)} %collective-permute-done.14.left_ref, f32[12288,384]{1,0:T(8,128)} %bitcast.45, f32[384,384]{1,0:T(8,128)} %broadcast_in_dim.14.total_ref), custom_call_target="tpu_custom_call" | custom-call | flops 1358954496 | bytes 4718592 | tf_op jit(solution)/shard_map/meet/pallas_call | solution.py:268
  62.6 107.6 %collective-permute-start.15 = (f32[512,384]{1,0:T(8,128)}, f32[512,384]{1,0:T(8,128)S(1)}, u32[]{:S(2)}, u32[]{:S(2)}) collective-permute-start(f32[512,384]{1,0:T(8,128)} %get-tuple-element.28), channel_id=1, source_target_pairs={{4,0},{8,4},{12,8},{5,1},{9,5},{13,9},{6,2},{10,6},{14,10},{7,3},{... | collective-permute-start | bytes 2359304 | tf_op jit(solution)/shard_map/ppermute | solution.py:361
  170.2 3.4 meet.19.total_ref
  173.6 8.0 %meet.16.total_ref = f32[384,384]{1,0:T(8,128)} custom-call(s32[4]{0:T(128)} %pad_add_fusion.at_ref, f32[2560,384]{1,0:T(8,128)} %collective-permute-done.13.left_ref, f32[12288,384]{1,0:T(8,128)} %bitcast.47, f32[384,384]{1,0:T(8,128)} %meet.15.total_ref), custom_call_target="tpu_custom_call" | custom-call | flops 2264924160 | bytes 7864320 | tf_op jit(solution)/shard_map/meet/pallas_call | solution.py:268
  181.6 5.9 %meet.17.total_ref = f32[384,384]{1,0:T(8,128)} custom-call(s32[4]{0:T(128)} %pad_add_fusion.at_ref, f32[1536,384]{1,0:T(8,128)} %copy-done.3, f32[12288,384]{1,0:T(8,128)} %bitcast.48, f32[384,384]{1,0:T(8,128)} %meet.16.total_ref), custom_call_target="tpu_custom_call" | custom-call | flops 1358954496 | bytes 4718592 | tf_op jit(solution)/shard_map/meet/pallas_call | solution.py:268
  187.5 4.2 %collective-permute-start.4 = (f32[8,128]{1,0:T(8,128)S(1)}, f32[8,128]{1,0:T(8,128)S(1)}, u32[]{:S(2)}, u32[]{:S(2)}) collective-permute-start(f32[8,128]{1,0:T(8,128)S(1)} %slice_add_fusion.1), channel_id=1, source_target_pairs={{0,4},{4,0},{8,12},{12,8},{1,5},{5,1},{9,13},{13,9},{2,6},{6,2},{1... | collective-permute-start | bytes 12296 | tf_op jit(solution)/shard_map/ppermute | solution.py:371
  191.7 3.8 %meet.18 = f32[384,384]{1,0:T(8,128)} custom-call(s32[4]{0:T(128)} %pad_add_fusion.at_ref, f32[512,384]{1,0:T(8,128)} %copy-done.8, f32[12288,384]{1,0:T(8,128)} %bitcast.49, f32[384,384]{1,0:T(8,128)} %meet.17.total_ref), custom_call_target="tpu_custom_call" | custom-call | flops 452984832 | bytes 1572864 | tf_op jit(solution)/shard_map/meet/pallas_call | solution.py:268
  195.5 3.4 meet.20.total_ref
  198.9 3.2 meet.21.total_ref
  202.9 3.1 meet.22
  207.3 3.4 collective-permute-start.18
  211.9 7.0 %meet.13.total_ref = f32[256,384]{1,0:T(8,128)} custom-call(s32[4]{0:T(128)} %pad_add_fusion.at_ref, f32[3072,256]{1,0:T(8,128)} %collective-permute-done.1.left_ref, f32[12288,384]{1,0:T(8,128)} %bitcast.53, f32[256,384]{1,0:T(8,128)} %broadcast_in_dim.12.total_ref, f32[8,128]{1,0:T(8,128)} %copy-done.9), custom_call_target="tpu_custom_call" | custom-call | flops 1811939328 | bytes 7864320 | tf_op jit(solution)/shard_map/meet/pallas_call | solution.py:268
  218.8 6.9 %meet.14.refs_0_ = f32[256,384]{1,0:T(8,128)} custom-call(s32[4]{0:T(128)} %pad_add_fusion.at_ref, f32[3072,256]{1,0:T(8,128)} %collective-permute-done.left_ref, f32[12288,384]{1,0:T(8,128)} %bitcast.54, f32[256,384]{1,0:T(8,128)} %meet.13.total_ref), custom_call_target="tpu_custom_call" | custom-call | flops 1811939328 | bytes 7864320 | tf_op jit(solution)/shard_map/meet/pallas_call | solution.py:268
  225.8 3.0 collective-permute-start.5
  228.8 3.2 collective-permute-done.19
  233.4 4.9 %collective-permute-done.5 = f32[256,384]{1,0:T(8,128)S(1)} collective-permute-done((f32[256,384]{1,0:T(8,128)}, f32[256,384]{1,0:T(8,128)S(1)}, u32[]{:S(2)}, u32[]{:S(2)}) %collective-permute-start.5) | collective-permute-done | bytes 393248 | tf_op jit(solution)/shard_map/ppermute | solution.py:144
  239.3 3.0 collective-permute-start.6
  242.3 1.6 collective-permute-start.24
  243.9 1.5 collective-permute-start.23
  245.9 12.7 %collective-permute-start.10 = (f32[2048,128]{1,0:T(8,128)}, f32[2048,128]{1,0:T(8,128)}, u32[]{:S(2)}, u32[]{:S(2)}) collective-permute-start(f32[2048,128]{1,0:T(8,128)} %get-tuple-element.23), channel_id=1, source_target_pairs={{0,12},{12,0},{1,13},{13,1},{2,14},{14,2},{3,15},{15,3},{16,28},{2... | collective-permute-start | bytes 3145736 | tf_op jit(solution)/shard_map/ppermute | solution.py:361
  258.7 3.8 %collective-permute-done.6 = f32[256,384]{1,0:T(8,128)S(1)} collective-permute-done((f32[256,384]{1,0:T(8,128)S(1)}, f32[256,384]{1,0:T(8,128)S(1)}, u32[]{:S(2)}, u32[]{:S(2)}) %collective-permute-start.6) | collective-permute-done | bytes 393248 | tf_op jit(solution)/shard_map/ppermute | solution.py:144
  262.5 8.7 %collective-permute-start.11 = (f32[3072,128]{1,0:T(8,128)}, f32[3072,128]{1,0:T(8,128)S(1)}, u32[]{:S(2)}, u32[]{:S(2)}) collective-permute-start(f32[3072,128]{1,0:T(8,128)} %get-tuple-element.24), channel_id=1, source_target_pairs={{0,12},{12,0},{1,13},{13,1},{2,14},{14,2},{3,15},{15,3},{16,28},{2... | collective-permute-start | bytes 4718600 | tf_op jit(solution)/shard_map/ppermute | solution.py:361
  271.2 1.5 collective-permute-start.7
  274.7 5.8 %polar.1 = f32[384,384]{1,0:T(8,128)} custom-call(f32[384,384]{1,0:T(8,128)} %pad_maximum_fusion.1.sum_ref, f32[256,384]{1,0:T(8,128)} %meet.14.refs_0_), custom_call_target="tpu_custom_call" | custom-call | tf_op jit(solution)/shard_map/polar/pallas_call | solution.py:54
  283.0 9.9 %collective-permute-done.7 = f32[256,384]{1,0:T(8,128)S(1)} collective-permute-done((f32[256,384]{1,0:T(8,128)S(1)}, f32[256,384]{1,0:T(8,128)S(1)}, u32[]{:S(2)}, u32[]{:S(2)}) %collective-permute-start.7) | collective-permute-done | bytes 393248 | tf_op jit(solution)/shard_map/ppermute | solution.py:190
  293.0 3.1 collective-permute-start.8
  296.0 1.9 collective-permute-start.9
  304.7 5.7 %meet.23.total_ref = f32[128,384]{1,0:T(8,128)} custom-call(s32[4]{0:T(128)} %pad_add_fusion.at_ref, f32[3072,128]{1,0:T(8,128)} %copy-done.5, f32[12288,384]{1,0:T(8,128)} %bitcast.55, f32[128,384]{1,0:T(8,128)} %broadcast_in_dim.13.total_ref, f32[96,384]{1,0:T(8,128)} %convolution_select_fusion.refs_0_, f32[256,384]{1,0:T(8,128)} %copy-done.2), custom_call_target="tpu_custom_call" | custom-call | flops 905969664 | bytes 6291456 | tf_op jit(solution)/shard_map/meet/pallas_call | solution.py:268
  310.4 4.2 %meet.24.total_ref = f32[128,384]{1,0:T(8,128)} custom-call(s32[4]{0:T(128)} %pad_add_fusion.at_ref, f32[2048,128]{1,0:T(8,128)} %collective-permute-done.10.left_ref, f32[12288,384]{1,0:T(8,128)} %bitcast.56, f32[128,384]{1,0:T(8,128)} %meet.23.total_ref, f32[256,384]{1,0:T(8,128)} %get-tuple-element.35.refs_0_, f32[256,384]{1,0:T(8,128)} %get-tuple-element.34.refs_1_), custom_call_target="tpu_custom_call" | custom-call | flops 603979776 | bytes 4194304 | tf_op jit(solution)/shard_map/meet/pallas_call | solution.py:268
  314.6 3.7 meet.25
  318.3 1.9 collective-permute-start.27
  320.2 7.6 %collective-permute-done.27 = f32[128,384]{1,0:T(8,128)S(1)} collective-permute-done((f32[128,384]{1,0:T(8,128)}, f32[128,384]{1,0:T(8,128)S(1)}, u32[]{:S(2)}, u32[]{:S(2)}) %collective-permute-start.27) | collective-permute-done | bytes 196640 | tf_op jit(solution)/shard_map/ppermute | solution.py:144
  328.7 2.6 collective-permute-start.28
  331.3 1.6 collective-permute-start.33
  335.0 6.2 %collective-permute-done.28 = f32[128,384]{1,0:T(8,128)S(1)} collective-permute-done((f32[128,384]{1,0:T(8,128)S(1)}, f32[128,384]{1,0:T(8,128)S(1)}, u32[]{:S(2)}, u32[]{:S(2)}) %collective-permute-start.28) | collective-permute-done | bytes 196640 | tf_op jit(solution)/shard_map/ppermute | solution.py:144
  341.2 1.5 collective-permute-start.29
  342.7 1.6 collective-permute-done.32
  348.2 22.3 %rotate.1 = f32[12288,384]{1,0:T(8,128)} custom-call(f32[384,384]{1,0:T(8,128)} %get-tuple-element.46.rows_ref, f32[384,384]{1,0:T(8,128)} %get-tuple-element.47.turned_ref, f32[384,384]{1,0:T(8,128)} %pad_maximum_fusion.5.later_ref, f32[12288,384]{1,0:T(8,128)} %bitcast.58), custom_call_target="tpu_custom_call" | custom-call | tf_op jit(solution)/shard_map/rotate/pallas_call | solution.py:118
  (90 shorter events, 31.7 us)
Async XLA Ops:
  3.8 23.7 %collective-permute-start.14 = (f32[1536,384]{1,0:T(8,128)}, f32[1536,384]{1,0:T(8,128)}, u32[]{:S(2)}, u32[]{:S(2)}) collective-permute-start(f32[1536,384]{1,0:T(8,128)} %get-tuple-element.27), channel_id=1, source_target_pairs={{0,4},{4,8},{8,12},{1,5},{5,9},{9,13},{2,6},{6,10},{10,14},{3,7},{... | collective-permute-start | bytes 7077896 | tf_op jit(solution)/shard_map/ppermute | solution.py:361
  5.1 40.6 %collective-permute-start.17 = (f32[1536,384]{1,0:T(8,128)}, f32[1536,384]{1,0:T(8,128)}, u32[]{:S(2)}, u32[]{:S(2)}) collective-permute-start(f32[1536,384]{1,0:T(8,128)} %get-tuple-element.30), channel_id=1, source_target_pairs={{4,0},{8,4},{12,8},{5,1},{9,5},{13,9},{6,2},{10,6},{14,10},{7,3},{... | collective-permute-start | bytes 7077896 | tf_op jit(solution)/shard_map/ppermute | solution.py:361
  13.7 34.0 %collective-permute-start.2 = (f32[1536,384]{1,0:T(8,128)}, f32[1536,384]{1,0:T(8,128)S(1)}, u32[]{:S(2)}, u32[]{:S(2)}) collective-permute-start(f32[1536,384]{1,0:T(8,128)} %get-tuple-element.20), channel_id=1, source_target_pairs={{0,4},{4,8},{8,12},{1,5},{5,9},{9,13},{2,6},{6,10},{10,14},{3,7},{... | collective-permute-start | bytes 7077896 | tf_op jit(solution)/shard_map/ppermute | solution.py:361
  20.6 42.0 %collective-permute-start.13 = (f32[2560,384]{1,0:T(8,128)}, f32[2560,384]{1,0:T(8,128)}, u32[]{:S(2)}, u32[]{:S(2)}) collective-permute-start(f32[2560,384]{1,0:T(8,128)} %get-tuple-element.26), channel_id=1, source_target_pairs={{0,4},{4,8},{8,12},{1,5},{5,9},{9,13},{2,6},{6,10},{10,14},{3,7},{... | collective-permute-start | bytes 11796488 | tf_op jit(solution)/shard_map/ppermute | solution.py:361
  21.9 173.6 %collective-permute-start.16 = (f32[2560,384]{1,0:T(8,128)}, f32[2560,384]{1,0:T(8,128)}, u32[]{:S(2)}, u32[]{:S(2)}) collective-permute-start(f32[2560,384]{1,0:T(8,128)} %get-tuple-element.29), channel_id=1, source_target_pairs={{4,0},{8,4},{12,8},{5,1},{9,5},{13,9},{6,2},{10,6},{14,10},{7,3},{... | collective-permute-start | bytes 11796488 | tf_op jit(solution)/shard_map/ppermute | solution.py:361
  27.5 26.9 %collective-permute-start.3 = (f32[1536,384]{1,0:T(8,128)}, f32[1536,384]{1,0:T(8,128)}, u32[]{:S(2)}, u32[]{:S(2)}) collective-permute-start(f32[1536,384]{1,0:T(8,128)} %get-tuple-element.21), channel_id=1, source_target_pairs={{4,0},{8,4},{12,8},{5,1},{9,5},{13,9},{6,2},{10,6},{14,10},{7,3},{... | collective-permute-start | bytes 7077896 | tf_op jit(solution)/shard_map/ppermute | solution.py:361
  45.8 165.3 %collective-permute-start.1 = (f32[3072,256]{1,0:T(8,128)}, f32[3072,256]{1,0:T(8,128)}, u32[]{:S(2)}, u32[]{:S(2)}) collective-permute-start(f32[3072,256]{1,0:T(8,128)} %get-tuple-element.19), channel_id=1, source_target_pairs={{0,12},{12,0},{1,13},{13,1},{2,14},{14,2},{3,15},{15,3},{16,28},{2... | collective-permute-start | bytes 9437192 | tf_op jit(solution)/shard_map/ppermute | solution.py:361
  47.7 14.2 %copy-start.3 = (f32[1536,384]{1,0:T(8,128)}, f32[1536,384]{1,0:T(8,128)S(1)}, u32[]{:S(2)}) copy-start(f32[1536,384]{1,0:T(8,128)S(1)} %collective-permute-done.2.left_ref) | copy-start | bytes 7077892
  47.7 171.1 %collective-permute-start = (f32[3072,256]{1,0:T(8,128)}, f32[3072,256]{1,0:T(8,128)}, u32[]{:S(2)}, u32[]{:S(2)}) collective-permute-start(f32[3072,256]{1,0:T(8,128)} %get-tuple-element.18), channel_id=1, source_target_pairs={{0,12},{12,0},{1,13},{13,1},{2,14},{14,2},{3,15},{15,3},{16,28},{2... | collective-permute-start | bytes 9437192 | tf_op jit(solution)/shard_map/ppermute | solution.py:361
  54.4 133.1 %collective-permute-start.12 = (f32[512,384]{1,0:T(8,128)}, f32[512,384]{1,0:T(8,128)S(1)}, u32[]{:S(2)}, u32[]{:S(2)}) collective-permute-start(f32[512,384]{1,0:T(8,128)} %get-tuple-element.25), channel_id=1, source_target_pairs={{0,4},{4,8},{8,12},{1,5},{5,9},{9,13},{2,6},{6,10},{10,14},{3,7},{... | collective-permute-start | bytes 2359304 | tf_op jit(solution)/shard_map/ppermute | solution.py:361
  62.6 139.4 %collective-permute-start.15 = (f32[512,384]{1,0:T(8,128)}, f32[512,384]{1,0:T(8,128)S(1)}, u32[]{:S(2)}, u32[]{:S(2)}) collective-permute-start(f32[512,384]{1,0:T(8,128)} %get-tuple-element.28), channel_id=1, source_target_pairs={{4,0},{8,4},{12,8},{5,1},{9,5},{13,9},{6,2},{10,6},{14,10},{7,3},{... | collective-permute-start | bytes 2359304 | tf_op jit(solution)/shard_map/ppermute | solution.py:361
  187.5 4.2 %copy-start.8 = (f32[512,384]{1,0:T(8,128)}, f32[512,384]{1,0:T(8,128)S(1)}, u32[]{:S(2)}) copy-start(f32[512,384]{1,0:T(8,128)S(1)} %collective-permute-done.12.left_ref) | copy-start | bytes 2359300
  187.5 23.2 %collective-permute-start.4 = (f32[8,128]{1,0:T(8,128)S(1)}, f32[8,128]{1,0:T(8,128)S(1)}, u32[]{:S(2)}, u32[]{:S(2)}) collective-permute-start(f32[8,128]{1,0:T(8,128)S(1)} %slice_add_fusion.1), channel_id=1, source_target_pairs={{0,4},{4,0},{8,12},{12,8},{1,5},{5,1},{9,13},{13,9},{2,6},{6,2},{1... | collective-permute-start | bytes 12296 | tf_op jit(solution)/shard_map/ppermute | solution.py:371
  202.0 4.0 %copy-start.4 = (f32[384,384]{1,0:T(8,128)S(1)}, f32[384,384]{1,0:T(8,128)}, u32[]{:S(2)}) copy-start(f32[384,384]{1,0:T(8,128)} %meet.18) | copy-start | bytes 1769476
  202.0 0.9 copy-start.7
  207.3 21.5 %collective-permute-start.18 = (f32[192,384]{1,0:T(8,128)S(1)}, f32[192,384]{1,0:T(8,128)S(1)}, u32[]{:S(2)}, u32[]{:S(2)}) collective-permute-start(f32[192,384]{1,0:T(8,128)S(1)} %get-tuple-element.31), channel_id=1, source_target_pairs={{0,3},{1,2},{2,1},{3,0},{4,7},{5,6},{6,5},{7,4},{8,11},{9,10},{10,... | collective-permute-start | bytes 884744 | tf_op jit(solution)/shard_map/ppermute | solution.py:144
  210.7 18.1 %collective-permute-start.20 = (f32[192,384]{1,0:T(8,128)S(1)}, f32[192,384]{1,0:T(8,128)S(1)}, u32[]{:S(2)}, u32[]{:S(2)}) collective-permute-start(f32[192,384]{1,0:T(8,128)S(1)} %get-tuple-element.32), channel_id=1, source_target_pairs={{0,1},{1,0},{2,3},{3,2},{4,5},{5,4},{6,7},{7,6},{8,9},{9,8},{10,11... | collective-permute-start | bytes 884744 | tf_op jit(solution)/shard_map/ppermute | solution.py:144
  210.7 1.1 copy-start.9
  210.7 21.3 %collective-permute-start.19 = (f32[192,384]{1,0:T(8,128)S(1)}, f32[192,384]{1,0:T(8,128)S(1)}, u32[]{:S(2)}, u32[]{:S(2)}) collective-permute-start(f32[192,384]{1,0:T(8,128)S(1)} %get-tuple-element.33), channel_id=1, source_target_pairs={{0,2},{1,3},{2,0},{3,1},{4,6},{5,7},{6,4},{7,5},{8,10},{9,11},{10,... | collective-permute-start | bytes 884744 | tf_op jit(solution)/shard_map/ppermute | solution.py:144
  225.8 12.5 %collective-permute-start.5 = (f32[256,384]{1,0:T(8,128)}, f32[256,384]{1,0:T(8,128)S(1)}, u32[]{:S(2)}, u32[]{:S(2)}) collective-permute-start(f32[256,384]{1,0:T(8,128)} %meet.14.refs_0_), channel_id=1, source_target_pairs={{0,1},{1,0},{2,3},{3,2},{12,13},{13,12},{14,15},{15,14},{16,17},{1... | collective-permute-start | bytes 1179656 | tf_op jit(solution)/shard_map/ppermute | solution.py:144
  232.1 10.2 %collective-permute-start.21 = (f32[96,384]{1,0:T(8,128)S(1)}, f32[96,384]{1,0:T(8,128)S(1)}, u32[]{:S(2)}, u32[]{:S(2)}) collective-permute-start(f32[96,384]{1,0:T(8,128)S(1)} %slice.19), channel_id=1, source_target_pairs={{0,4},{4,8},{8,12},{1,5},{5,9},{9,13},{2,6},{6,10},{10,14},{3,7},{... | collective-permute-start | bytes 442376 | tf_op jit(solution)/shard_map/ppermute | solution.py:389
  239.3 35.4 %copy-start.2 = (f32[256,384]{1,0:T(8,128)}, f32[256,384]{1,0:T(8,128)S(1)}, u32[]{:S(2)}) copy-start(f32[256,384]{1,0:T(8,128)S(1)} %add.60.refs_1_) | copy-start | bytes 1179652
  239.3 23.2 %collective-permute-start.6 = (f32[256,384]{1,0:T(8,128)S(1)}, f32[256,384]{1,0:T(8,128)S(1)}, u32[]{:S(2)}, u32[]{:S(2)}) collective-permute-start(f32[256,384]{1,0:T(8,128)S(1)} %add.60.refs_1_), channel_id=1, source_target_pairs={{0,2},{1,3},{2,0},{3,1},{12,14},{13,15},{14,12},{15,13},{16,18},{1... | collective-permute-start | bytes 1179656 | tf_op jit(solution)/shard_map/ppermute | solution.py:144
  242.3 28.9 %collective-permute-start.24 = (f32[96,384]{1,0:T(8,128)S(1)}, f32[96,384]{1,0:T(8,128)S(1)}, u32[]{:S(2)}, u32[]{:S(2)}) collective-permute-start(f32[96,384]{1,0:T(8,128)S(1)} %slice_add_fusion), channel_id=1, source_target_pairs={{0,3},{1,2},{2,1},{3,0},{4,7},{5,6},{6,5},{7,4},{8,11},{9,10},{10,... | collective-permute-start | bytes 442376 | tf_op jit(solution)/shard_map/ppermute | solution.py:144
  243.9 28.8 %collective-permute-start.23 = (f32[96,384]{1,0:T(8,128)S(1)}, f32[96,384]{1,0:T(8,128)}, u32[]{:S(2)}, u32[]{:S(2)}) collective-permute-start(f32[96,384]{1,0:T(8,128)S(1)} %slice_add_fusion), channel_id=1, source_target_pairs={{0,2},{1,3},{2,0},{3,1},{4,6},{5,7},{6,4},{7,5},{8,10},{9,11},{10,... | collective-permute-start | bytes 442376 | tf_op jit(solution)/shard_map/ppermute | solution.py:144
  245.4 27.3 %collective-permute-start.22 = (f32[96,384]{1,0:T(8,128)S(1)}, f32[96,384]{1,0:T(8,128)}, u32[]{:S(2)}, u32[]{:S(2)}) collective-permute-start(f32[96,384]{1,0:T(8,128)S(1)} %slice_add_fusion), channel_id=1, source_target_pairs={{0,1},{1,0},{2,3},{3,2},{4,5},{5,4},{6,7},{7,6},{8,9},{9,8},{10,11... | collective-permute-start | bytes 442376 | tf_op jit(solution)/shard_map/ppermute | solution.py:144
  245.9 64.5 %collective-permute-start.10 = (f32[2048,128]{1,0:T(8,128)}, f32[2048,128]{1,0:T(8,128)}, u32[]{:S(2)}, u32[]{:S(2)}) collective-permute-start(f32[2048,128]{1,0:T(8,128)} %get-tuple-element.23), channel_id=1, source_target_pairs={{0,12},{12,0},{1,13},{13,1},{2,14},{14,2},{3,15},{15,3},{16,28},{2... | collective-permute-start | bytes 3145736 | tf_op jit(solution)/shard_map/ppermute | solution.py:361
  262.5 41.0 %collective-permute-start.11 = (f32[3072,128]{1,0:T(8,128)}, f32[3072,128]{1,0:T(8,128)S(1)}, u32[]{:S(2)}, u32[]{:S(2)}) collective-permute-start(f32[3072,128]{1,0:T(8,128)} %get-tuple-element.24), channel_id=1, source_target_pairs={{0,12},{12,0},{1,13},{13,1},{2,14},{14,2},{3,15},{15,3},{16,28},{2... | collective-permute-start | bytes 4718600 | tf_op jit(solution)/shard_map/ppermute | solution.py:361
  271.2 21.7 %collective-permute-start.7 = (f32[256,384]{1,0:T(8,128)S(1)}, f32[256,384]{1,0:T(8,128)S(1)}, u32[]{:S(2)}, u32[]{:S(2)}) collective-permute-start(f32[256,384]{1,0:T(8,128)S(1)} %add.61), channel_id=1, source_target_pairs={{0,8},{12,4},{1,9},{13,5},{2,10},{14,6},{3,11},{15,7},{16,24},{28,... | collective-permute-start | bytes 1179656 | tf_op jit(solution)/shard_map/ppermute | solution.py:190
  281.6 16.3 %collective-permute-start.25 = (f32[96,384]{1,0:T(8,128)S(1)}, f32[96,384]{1,0:T(8,128)}, u32[]{:S(2)}, u32[]{:S(2)}) collective-permute-start(f32[96,384]{1,0:T(8,128)S(1)} %constant_dynamic-slice_fusion), channel_id=1, source_target_pairs={{4,8},{5,9},{6,10},{7,11},{20,24},{21,25},{22,26},{23,27}} | collective-permute-start | bytes 442376 | tf_op jit(solution)/shard_map/ppermute | solution.py:401
  293.0 7.6 %collective-permute-start.8 = (f32[256,384]{1,0:T(8,128)S(1)}, f32[256,384]{1,0:T(8,128)S(1)}, u32[]{:S(2)}, u32[]{:S(2)}) collective-permute-start(f32[256,384]{1,0:T(8,128)S(1)} %broadcast_select_fusion), channel_id=1, source_target_pairs={{0,4},{4,0},{8,12},{12,8},{1,5},{5,1},{9,13},{13,9},{2,6},{6,2},{1... | collective-permute-start | bytes 1179656 | tf_op jit(solution)/shard_map/ppermute | solution.py:192
  296.0 18.6 %collective-permute-start.9 = (f32[1024,128]{1,0:T(8,128)}, f32[1024,128]{1,0:T(8,128)}, u32[]{:S(2)}, u32[]{:S(2)}) collective-permute-start(f32[1024,128]{1,0:T(8,128)} %get-tuple-element.22), channel_id=1, source_target_pairs={{0,12},{12,0},{1,13},{13,1},{2,14},{14,2},{3,15},{15,3},{16,28},{2... | collective-permute-start | bytes 1572872 | tf_op jit(solution)/shard_map/ppermute | solution.py:361
  299.2 3.3 collective-permute-start.26
  303.5 1.2 copy-start.5
  314.6 16.7 %copy-start.6 = (f32[96,384]{1,0:T(8,128)S(1)}, f32[96,384]{1,0:T(8,128)}, u32[]{:S(2)}) copy-start(f32[96,384]{1,0:T(8,128)} %convolution_select_fusion.refs_0_) | copy-start | bytes 442372
  318.3 9.5 %collective-permute-start.27 = (f32[128,384]{1,0:T(8,128)}, f32[128,384]{1,0:T(8,128)S(1)}, u32[]{:S(2)}, u32[]{:S(2)}) collective-permute-start(f32[128,384]{1,0:T(8,128)} %meet.25), channel_id=1, source_target_pairs={{0,1},{1,0},{2,3},{3,2},{12,13},{13,12},{14,15},{15,14},{16,17},{1... | collective-permute-start | bytes 589832 | tf_op jit(solution)/shard_map/ppermute | solution.py:144
  328.7 12.4 %collective-permute-start.28 = (f32[128,384]{1,0:T(8,128)S(1)}, f32[128,384]{1,0:T(8,128)S(1)}, u32[]{:S(2)}, u32[]{:S(2)}) collective-permute-start(f32[128,384]{1,0:T(8,128)S(1)} %add.75), channel_id=1, source_target_pairs={{0,2},{1,3},{2,0},{3,1},{12,14},{13,15},{14,12},{15,13},{16,18},{1... | collective-permute-start | bytes 589832 | tf_op jit(solution)/shard_map/ppermute | solution.py:144
  331.3 11.4 %collective-permute-start.33 = (f32[96,384]{1,0:T(8,128)S(1)}, f32[96,384]{1,0:T(8,128)S(1)}, u32[]{:S(2)}, u32[]{:S(2)}) collective-permute-start(f32[96,384]{1,0:T(8,128)S(1)} %copy-done.6), channel_id=1, source_target_pairs={{0,3},{1,2},{2,1},{3,0},{4,7},{5,6},{6,5},{7,4},{8,11},{9,10},{10,... | collective-permute-start | bytes 442376 | tf_op jit(solution)/shard_map/ppermute | solution.py:144
  332.9 11.4 %collective-permute-start.32 = (f32[96,384]{1,0:T(8,128)S(1)}, f32[96,384]{1,0:T(8,128)S(1)}, u32[]{:S(2)}, u32[]{:S(2)}) collective-permute-start(f32[96,384]{1,0:T(8,128)S(1)} %copy-done.6), channel_id=1, source_target_pairs={{0,2},{1,3},{2,0},{3,1},{4,6},{5,7},{6,4},{7,5},{8,10},{9,11},{10,... | collective-permute-start | bytes 442376 | tf_op jit(solution)/shard_map/ppermute | solution.py:144
  334.4 9.9 %collective-permute-start.31 = (f32[96,384]{1,0:T(8,128)S(1)}, f32[96,384]{1,0:T(8,128)S(1)}, u32[]{:S(2)}, u32[]{:S(2)}) collective-permute-start(f32[96,384]{1,0:T(8,128)S(1)} %copy-done.6), channel_id=1, source_target_pairs={{0,1},{1,0},{2,3},{3,2},{4,5},{5,4},{6,7},{7,6},{8,9},{9,8},{10,11... | collective-permute-start | bytes 442376 | tf_op jit(solution)/shard_map/ppermute | solution.py:144
  341.2 3.9 %collective-permute-start.29 = (f32[128,384]{1,0:T(8,128)S(1)}, f32[128,384]{1,0:T(8,128)S(1)}, u32[]{:S(2)}, u32[]{:S(2)}) collective-permute-start(f32[128,384]{1,0:T(8,128)S(1)} %add.76), channel_id=1, source_target_pairs={{0,8},{12,4},{1,9},{13,5},{2,10},{14,6},{3,11},{15,7},{16,24},{28,... | collective-permute-start | bytes 589832 | tf_op jit(solution)/shard_map/ppermute | solution.py:190
  344.3 2.8 copy-start
  344.3 2.8 copy-start.1
  345.1 2.0 collective-permute-start.30
where the time goes:
time: 374 us; the launch traced here: 371 us
  starting transfers between devices  199 us (53%)
  Pallas kernels  115 us (31%)
  waiting for transfers between devices  39.1 us (10%)
  other arithmetic  10.6 us (3%)
  local copies, waits for them, and re-layouts  4.03 us (1%)
    ppermute x13, starting transfers between devices, stream(): streamed.append(tuple((lax.ppermute(x, 'ka', way) for x, way in pieces)))  163 us
    pallas_call x13, Pallas kernels, meet(): pl.pallas_call(functools.partial(meet_kernel, flag), out_shape=jax.ShapeD...  63.6 us
    ppermute x13, waiting for transfers between devices, xor_permute(): return lax.ppermute(x, ('ka', 'coef'), route)  27.2 us
    pallas_call x1, Pallas kernels, rotate_call(): pl.pallas_call(functools.partial(rotate_kernel, total), out_shape=jax.Sha...  22.3 us
    ppermute x13, starting transfers between devices, xor_permute(): return lax.ppermute(x, ('ka', 'coef'), route)  21.5 us
    pallas_call x4, Pallas kernels, copy_rows(): pl.pallas_call(functools.partial(copy_rows_kernel, pieces), out_shape=[ja...  15.7 us
    ppermute x2, waiting for transfers between devices, ends(): across = lax.ppermute(x, 'ka', [(0, 2), (3, 1)])  10.7 us
  transfers between devices with their start and end apart: 34, of which 10 were waited for; matrix products, arithmetic and copies ran while one was open for 4% of the time, Pallas kernels for 23%

commit v1 on v0

--- a/solution.py
+++ b/solution.py
@@ -133,8 +133,8 @@
     )(rows, turned, later, wave)
 
 
-def few(axis):
-    return lax.axis_size(axis) in (2, 4)
+def few(axis, mesh=None):
+    return (mesh.shape[axis] if mesh else lax.axis_size(axis)) in (2, 4)
 
 
 def xor_permute(x, distance, ends_only=False):
@@ -171,10 +171,11 @@
     )
 
 
-def end_sum(x, distance=1):
+def end_sum(x):
     count = lax.axis_size("coef")
     if not few("coef"):
         return lax.psum(x, "coef")
+    distance = 1
     while distance < count:
         x = x + xor_permute(x, distance, True)
         distance *= 2
@@ -336,7 +337,7 @@
 
 FIRSTS = (3, 5, 3, 1)
 WIDES = (6, 6)
-LATES = (6, 4, 2)
+LATES = (6, 5, 1)
 
 
 def whole_step(wavefunctions):
@@ -391,7 +392,8 @@
     first = len(firsts)
     early = close(first, wides[0], early, token)
     early = close(first + 1, wides[1], early)
-    unitary = polar_call(gather_rows(margin_share), total, early)
+    margin = gather_rows(margin_share)
+    unitary = polar_call(margin, total, early)
 
     mine = lax.axis_index("coef")
     share = size // coefs
@@ -403,10 +405,9 @@
         product = jnp.where(position == k + 1, longer, product)
     later = gather_rows(product)
 
-    pair = early + xor_permute(early, 1, True) if few("coef") else early
-    late = close(first + 2, lates[0], jnp.zeros((128, size), F32), product, pair)
-    early = ends(end_sum(pair, 2) if few("coef") else end_sum(early))
-    late = close(first + 3, lates[1], late, *early)
+    early = ends(end_sum(early))
+    late = close(first + 2, lates[0], jnp.zeros((128, size), F32))
+    late = close(first + 3, lates[1], late)
     late = close(first + 4, lates[2], late)
     late = ends(end_sum(late))
     rows, turned = [jnp.concatenate(pair) for pair in zip(early, late)]

time: 374 us -> 366 us (0.979)
  starting transfers between devices: 199 us -> 165 us
  waiting for transfers between devices: 39.1 us -> 69.2 us
    ppermute x13, starting transfers between devices: 163 us -> 123 us  [stream(): streamed.append(tuple((lax.ppermute(x, 'ka', way) for x, way in pieces)))]
    ppermute x13, waiting for transfers between devices: 0.03 us -> 33.8 us  [stream(): streamed.append(tuple((lax.ppermute(x, 'ka', way) for x, way in pieces)))]
    ppermute x2, starting transfers between devices: 3.02 us -> 14.9 us  [ends(): across = lax.ppermute(x, 'ka', [(0, 2), (3, 1)])]
    ppermute x2, waiting for transfers between devices: 10.7 us -> 0.01 us  [ends(): across = lax.ppermute(x, 'ka', [(0, 2), (3, 1)])]
    ppermute x13, waiting for transfers between devices: 27.2 us -> 33.5 us  [xor_permute(): return lax.ppermute(x, ('ka', 'coef'), route)]
    ppermute x2, starting transfers between devices: 3.98 us -> 0.14 us  [ends(): other = lax.ppermute(own, 'ka', [(0, 1), (1, 0), (2, 3), (3, 2)])]
  transfers between devices with their start and end apart: 34 -> 34, of which waited for: 10 -> 8; matrix products, arithmetic and copies ran while one was open for 4% -> 3% of each run, Pallas kernels for 23% -> 24%
where the time goes in v1:
time: 366 us; the launch traced here: 364 us
  starting transfers between devices  165 us (45%)
  Pallas kernels  116 us (32%)
  waiting for transfers between devices  69.2 us (19%)
  other arithmetic  7.95 us (2%)
  local copies, waits for them, and re-layouts  4.21 us (1%)
    ppermute x13, starting transfers between devices, stream(): streamed.append(tuple((lax.ppermute(x, 'ka', way) for x, way in pieces)))  123 us
    pallas_call x13, Pallas kernels, meet(): pl.pallas_call(functools.partial(meet_kernel, flag), out_shape=jax.ShapeD...  64.9 us
    ppermute x13, waiting for transfers between devices, stream(): streamed.append(tuple((lax.ppermute(x, 'ka', way) for x, way in pieces)))  33.8 us
    ppermute x13, waiting for transfers between devices, xor_permute(): return lax.ppermute(x, ('ka', 'coef'), route)  33.5 us
    ppermute x13, starting transfers between devices, xor_permute(): return lax.ppermute(x, ('ka', 'coef'), route)  23.7 us
    pallas_call x1, Pallas kernels, rotate_call(): pl.pallas_call(functools.partial(rotate_kernel, total), out_shape=jax.Sha...  22.3 us
    pallas_call x4, Pallas kernels, copy_rows(): pl.pallas_call(functools.partial(copy_rows_kernel, pieces), out_shape=[ja...  15.8 us
    ppermute x2, starting transfers between devices, ends(): across = lax.ppermute(x, 'ka', [(0, 2), (3, 1)])  14.9 us
  transfers between devices with their start and end apart: 34, of which 8 were waited for; matrix products, arithmetic and copies ran while one was open for 3% of the time, Pallas kernels for 24%

profile of v1, /device:TPU:7, one launch (start us, length us, event | category | flops | bytes accessed | tf_op | source)
XLA Modules:
  0.0 364.3 jit_solution(2109549339804828033)
XLA Ops:
  0.0 7.5 %cut.1 = (f32[3072,256]{1,0:T(8,128)}, f32[3072,256]{1,0:T(8,128)}, f32[3072,128]{1,0:T(8,128)}, f32[2560,128]{1,0:T(8,128)}, f32[512,128]{1,0:T(8,128)}) custom-call(s32[1]{0:T(128)} %bitcast.4.start, f32[12288,384]{1,0:T(8,128)} %bitcast.40), custom_call_target="tpu_custom_call" | custom-call | tf_op jit(solution)/shard_map/cut/pallas_call | solution.py:324
  7.5 2.7 collective-permute-start.11
  10.3 2.8 collective-permute-start.10
  13.1 3.8 %copy_rows.7 = (f32[1536,384]{1,0:T(8,128)}, f32[1536,384]{1,0:T(8,128)}) custom-call(f32[12288,384]{1,0:T(8,128)} %bitcast.41), custom_call_target="tpu_custom_call" | custom-call | tf_op jit(solution)/shard_map/copy_rows/pallas_call | solution.py:219
  18.2 4.5 %collective-permute-start.21 = (f32[1536,384]{1,0:T(8,128)}, f32[1536,384]{1,0:T(8,128)}, u32[]{:S(2)}, u32[]{:S(2)}) collective-permute-start(f32[1536,384]{1,0:T(8,128)} %get-tuple-element.30), channel_id=1, source_target_pairs={{4,0},{8,4},{12,8},{5,1},{9,5},{13,9},{6,2},{10,6},{14,10},{7,3},{... | collective-permute-start | bytes 7077896 | tf_op jit(solution)/shard_map/ppermute | solution.py:362
  22.8 3.9 %copy_rows.4 = (f32[1536,384]{1,0:T(8,128)}, f32[1536,384]{1,0:T(8,128)}) custom-call(f32[12288,384]{1,0:T(8,128)} %bitcast.42), custom_call_target="tpu_custom_call" | custom-call | tf_op jit(solution)/shard_map/copy_rows/pallas_call | solution.py:219
  26.6 1.4 collective-permute-start.2
  28.1 5.7 %copy_rows.6 = (f32[2560,384]{1,0:T(8,128)}, f32[2560,384]{1,0:T(8,128)}) custom-call(f32[12288,384]{1,0:T(8,128)} %bitcast.43), custom_call_target="tpu_custom_call" | custom-call | tf_op jit(solution)/shard_map/copy_rows/pallas_call | solution.py:219
  33.7 33.7 %collective-permute-done.10.left_ref = f32[2560,128]{1,0:T(8,128)} collective-permute-done((f32[2560,128]{1,0:T(8,128)}, f32[2560,128]{1,0:T(8,128)}, u32[]{:S(2)}, u32[]{:S(2)}) %collective-permute-start.10) | collective-permute-done | bytes 1310752 | tf_op jit(solution)/shard_map/ppermute | solution.py:362
  68.8 3.3 collective-permute-start.9
  73.5 5.7 %meet.15.total_ref = f32[128,384]{1,0:T(8,128)} custom-call(s32[4]{0:T(128)} %pad_add_fusion.at_ref, f32[3072,128]{1,0:T(8,128)} %collective-permute-done.11.left_ref, f32[12288,384]{1,0:T(8,128)} %bitcast.44, f32[128,384]{1,0:T(8,128)} %broadcast_in_dim.13.total_ref), custom_call_target="tpu_custom_call" | custom-call | flops 905969664 | bytes 6291456 | tf_op jit(solution)/shard_map/meet/pallas_call | solution.py:269
  79.2 6.2 %meet.16.total_ref = f32[128,384]{1,0:T(8,128)} custom-call(s32[4]{0:T(128)} %pad_add_fusion.at_ref, f32[2560,128]{1,0:T(8,128)} %collective-permute-done.10.left_ref, f32[12288,384]{1,0:T(8,128)} %bitcast.45, f32[128,384]{1,0:T(8,128)} %meet.15.total_ref), custom_call_target="tpu_custom_call" | custom-call | flops 754974720 | bytes 5242880 | tf_op jit(solution)/shard_map/meet/pallas_call | solution.py:269
  86.1 3.0 meet.17
  89.1 3.2 collective-permute-start.12
  92.3 3.7 %collective-permute-done.12 = f32[128,384]{1,0:T(8,128)S(1)} collective-permute-done((f32[128,384]{1,0:T(8,128)}, f32[128,384]{1,0:T(8,128)S(1)}, u32[]{:S(2)}, u32[]{:S(2)}) %collective-permute-start.12) | collective-permute-done | bytes 196640 | tf_op jit(solution)/shard_map/ppermute | solution.py:144
  96.0 3.2 collective-permute-start.20
  99.2 2.7 collective-permute-start.3
  101.9 1.9 collective-permute-start.1
  103.8 3.6 collective-permute-start
  107.5 2.4 copy_rows.5
  112.2 5.3 %meet.18.total_ref = f32[384,384]{1,0:T(8,128)} custom-call(s32[4]{0:T(128)} %pad_add_fusion.at_ref, f32[1536,384]{1,0:T(8,128)} %collective-permute-done.18.left_ref, f32[12288,384]{1,0:T(8,128)} %bitcast.48, f32[384,384]{1,0:T(8,128)} %broadcast_in_dim.14.total_ref), custom_call_target="tpu_custom_call" | custom-call | flops 1358954496 | bytes 4718592 | tf_op jit(solution)/shard_map/meet/pallas_call | solution.py:269
  118.2 92.4 %collective-permute-start.19 = (f32[512,384]{1,0:T(8,128)}, f32[512,384]{1,0:T(8,128)S(1)}, u32[]{:S(2)}, u32[]{:S(2)}) collective-permute-start(f32[512,384]{1,0:T(8,128)} %get-tuple-element.28), channel_id=1, source_target_pairs={{4,0},{8,4},{12,8},{5,1},{9,5},{13,9},{6,2},{10,6},{14,10},{7,3},{... | collective-permute-start | bytes 2359304 | tf_op jit(solution)/shard_map/ppermute | solution.py:362
  210.6 3.4 meet.22.total_ref
  214.0 8.0 %meet.19.total_ref = f32[384,384]{1,0:T(8,128)} custom-call(s32[4]{0:T(128)} %pad_add_fusion.at_ref, f32[2560,384]{1,0:T(8,128)} %collective-permute-done.17.left_ref, f32[12288,384]{1,0:T(8,128)} %bitcast.50, f32[384,384]{1,0:T(8,128)} %meet.18.total_ref), custom_call_target="tpu_custom_call" | custom-call | flops 2264924160 | bytes 7864320 | tf_op jit(solution)/shard_map/meet/pallas_call | solution.py:269
  222.0 5.9 %meet.20.total_ref = f32[384,384]{1,0:T(8,128)} custom-call(s32[4]{0:T(128)} %pad_add_fusion.at_ref, f32[1536,384]{1,0:T(8,128)} %copy-done.1, f32[12288,384]{1,0:T(8,128)} %bitcast.51, f32[384,384]{1,0:T(8,128)} %meet.19.total_ref), custom_call_target="tpu_custom_call" | custom-call | flops 1358954496 | bytes 4718592 | tf_op jit(solution)/shard_map/meet/pallas_call | solution.py:269
  228.0 4.2 %collective-permute-start.13 = (f32[128,384]{1,0:T(8,128)S(1)}, f32[128,384]{1,0:T(8,128)S(1)}, u32[]{:S(2)}, u32[]{:S(2)}) collective-permute-start(f32[128,384]{1,0:T(8,128)S(1)} %add.62), channel_id=1, source_target_pairs={{0,2},{1,3},{2,0},{3,1},{12,14},{13,15},{14,12},{15,13},{16,18},{1... | collective-permute-start | bytes 589832 | tf_op jit(solution)/shard_map/ppermute | solution.py:144
  232.2 3.8 %meet.21 = f32[384,384]{1,0:T(8,128)} custom-call(s32[4]{0:T(128)} %pad_add_fusion.at_ref, f32[512,384]{1,0:T(8,128)} %copy-done.5, f32[12288,384]{1,0:T(8,128)} %bitcast.52, f32[384,384]{1,0:T(8,128)} %meet.20.total_ref), custom_call_target="tpu_custom_call" | custom-call | flops 452984832 | bytes 1572864 | tf_op jit(solution)/shard_map/meet/pallas_call | solution.py:269
  236.8 3.4 meet.23.total_ref
  240.2 3.2 meet.24.total_ref
  244.3 3.1 meet.25
  248.7 3.4 collective-permute-start.22
  253.2 6.9 %meet.13.total_ref = f32[256,384]{1,0:T(8,128)} custom-call(s32[4]{0:T(128)} %pad_add_fusion.at_ref, f32[3072,256]{1,0:T(8,128)} %collective-permute-done.1.left_ref, f32[12288,384]{1,0:T(8,128)} %bitcast.56, f32[256,384]{1,0:T(8,128)} %broadcast_in_dim.12.total_ref, f32[8,128]{1,0:T(8,128)} %copy-done.7), custom_call_target="tpu_custom_call" | custom-call | flops 1811939328 | bytes 7864320 | tf_op jit(solution)/shard_map/meet/pallas_call | solution.py:269
  260.1 6.9 %meet.14.refs_0_ = f32[256,384]{1,0:T(8,128)} custom-call(s32[4]{0:T(128)} %pad_add_fusion.at_ref, f32[3072,256]{1,0:T(8,128)} %collective-permute-done.left_ref, f32[12288,384]{1,0:T(8,128)} %bitcast.57, f32[256,384]{1,0:T(8,128)} %meet.13.total_ref), custom_call_target="tpu_custom_call" | custom-call | flops 1811939328 | bytes 7864320 | tf_op jit(solution)/shard_map/meet/pallas_call | solution.py:269
  267.0 3.3 collective-permute-start.5
  270.4 3.0 collective-permute-done.23
  275.9 13.5 %collective-permute-start.14 = (f32[128,384]{1,0:T(8,128)S(1)}, f32[128,384]{1,0:T(8,128)S(1)}, u32[]{:S(2)}, u32[]{:S(2)}) collective-permute-start(f32[128,384]{1,0:T(8,128)S(1)} %add.63), channel_id=1, source_target_pairs={{0,8},{12,4},{1,9},{13,5},{2,10},{14,6},{3,11},{15,7},{16,24},{28,... | collective-permute-start | bytes 589832 | tf_op jit(solution)/shard_map/ppermute | solution.py:191
  289.5 1.9 collective-permute-start.6
  291.5 2.3 collective-permute-start.28
  293.8 1.5 collective-permute-start.27
  295.3 15.6 %collective-permute-done.6 = f32[256,384]{1,0:T(8,128)S(1)} collective-permute-done((f32[256,384]{1,0:T(8,128)S(1)}, f32[256,384]{1,0:T(8,128)S(1)}, u32[]{:S(2)}, u32[]{:S(2)}) %collective-permute-start.6) | collective-permute-done | bytes 393248 | tf_op jit(solution)/shard_map/ppermute | solution.py:144
  310.9 1.3 collective-permute-start.7
  312.3 1.8 collective-permute-done.27
  315.0 5.8 %polar.1 = f32[384,384]{1,0:T(8,128)} custom-call(f32[384,384]{1,0:T(8,128)} %pad_maximum_fusion.3.sum_ref, f32[256,384]{1,0:T(8,128)} %meet.14.refs_0_), custom_call_target="tpu_custom_call" | custom-call | tf_op jit(solution)/shard_map/polar/pallas_call | solution.py:54
  324.5 1.9 collective-permute-done.30
  327.9 2.5 collective-permute-start.31
  331.6 2.3 collective-permute-done.33
  333.9 7.0 %collective-permute-done.32 = f32[96,384]{1,0:T(8,128)S(1)} collective-permute-done((f32[96,384]{1,0:T(8,128)S(1)}, f32[96,384]{1,0:T(8,128)S(1)}, u32[]{:S(2)}, u32[]{:S(2)}) %collective-permute-start.32) | collective-permute-done | bytes 147488 | tf_op jit(solution)/shard_map/ppermute | solution.py:144
  341.9 22.3 %rotate.1 = f32[12288,384]{1,0:T(8,128)} custom-call(f32[384,384]{1,0:T(8,128)} %get-tuple-element.46.rows_ref, f32[384,384]{1,0:T(8,128)} %get-tuple-element.47.turned_ref, f32[384,384]{1,0:T(8,128)} %pad_maximum_fusion.5.later_ref, f32[12288,384]{1,0:T(8,128)} %bitcast.58), custom_call_target="tpu_custom_call" | custom-call | tf_op jit(solution)/shard_map/rotate/pallas_call | solution.py:118
  (88 shorter events, 22.4 us)
Async XLA Ops:
  7.5 61.3 %collective-permute-start.11 = (f32[3072,128]{1,0:T(8,128)}, f32[3072,128]{1,0:T(8,128)}, u32[]{:S(2)}, u32[]{:S(2)}) collective-permute-start(f32[3072,128]{1,0:T(8,128)} %get-tuple-element.24), channel_id=1, source_target_pairs={{0,12},{12,0},{1,13},{13,1},{2,14},{14,2},{3,15},{15,3},{16,28},{2... | collective-permute-start | bytes 4718600 | tf_op jit(solution)/shard_map/ppermute | solution.py:362
  10.3 57.2 %collective-permute-start.10 = (f32[2560,128]{1,0:T(8,128)}, f32[2560,128]{1,0:T(8,128)}, u32[]{:S(2)}, u32[]{:S(2)}) collective-permute-start(f32[2560,128]{1,0:T(8,128)} %get-tuple-element.23), channel_id=1, source_target_pairs={{0,12},{12,0},{1,13},{13,1},{2,14},{14,2},{3,15},{15,3},{16,28},{2... | collective-permute-start | bytes 3932168 | tf_op jit(solution)/shard_map/ppermute | solution.py:362
  16.9 82.3 %collective-permute-start.18 = (f32[1536,384]{1,0:T(8,128)}, f32[1536,384]{1,0:T(8,128)}, u32[]{:S(2)}, u32[]{:S(2)}) collective-permute-start(f32[1536,384]{1,0:T(8,128)} %get-tuple-element.27), channel_id=1, source_target_pairs={{0,4},{4,8},{8,12},{1,5},{5,9},{9,13},{2,6},{6,10},{10,14},{3,7},{... | collective-permute-start | bytes 7077896 | tf_op jit(solution)/shard_map/ppermute | solution.py:362
  18.2 83.6 %collective-permute-start.21 = (f32[1536,384]{1,0:T(8,128)}, f32[1536,384]{1,0:T(8,128)}, u32[]{:S(2)}, u32[]{:S(2)}) collective-permute-start(f32[1536,384]{1,0:T(8,128)} %get-tuple-element.30), channel_id=1, source_target_pairs={{4,0},{8,4},{12,8},{5,1},{9,5},{13,9},{6,2},{10,6},{14,10},{7,3},{... | collective-permute-start | bytes 7077896 | tf_op jit(solution)/shard_map/ppermute | solution.py:362
  26.6 42.2 %copy-start.8 = (f32[512,128]{1,0:T(8,128)S(1)}, f32[512,128]{1,0:T(8,128)}, u32[]{:S(2)}) copy-start(f32[512,128]{1,0:T(8,128)} %get-tuple-element.22) | copy-start | bytes 786436
  26.6 77.2 %collective-permute-start.2 = (f32[1536,384]{1,0:T(8,128)}, f32[1536,384]{1,0:T(8,128)S(1)}, u32[]{:S(2)}, u32[]{:S(2)}) collective-permute-start(f32[1536,384]{1,0:T(8,128)} %get-tuple-element.20), channel_id=1, source_target_pairs={{0,4},{4,8},{8,12},{1,5},{5,9},{9,13},{2,6},{6,10},{10,14},{3,7},{... | collective-permute-start | bytes 7077896 | tf_op jit(solution)/shard_map/ppermute | solution.py:362
  67.5 50.7 %collective-permute-start.17 = (f32[2560,384]{1,0:T(8,128)}, f32[2560,384]{1,0:T(8,128)}, u32[]{:S(2)}, u32[]{:S(2)}) collective-permute-start(f32[2560,384]{1,0:T(8,128)} %get-tuple-element.26), channel_id=1, source_target_pairs={{0,4},{4,8},{8,12},{1,5},{5,9},{9,13},{2,6},{6,10},{10,14},{3,7},{... | collective-permute-start | bytes 11796488 | tf_op jit(solution)/shard_map/ppermute | solution.py:362
  68.8 16.6 %collective-permute-start.9 = (f32[512,128]{1,0:T(8,128)S(1)}, f32[512,128]{1,0:T(8,128)S(1)}, u32[]{:S(2)}, u32[]{:S(2)}) collective-permute-start(f32[512,128]{1,0:T(8,128)S(1)} %copy-done.8), channel_id=1, source_target_pairs={{0,12},{12,0},{1,13},{13,1},{2,14},{14,2},{3,15},{15,3},{16,28},{2... | collective-permute-start | bytes 786440 | tf_op jit(solution)/shard_map/ppermute | solution.py:362
  85.4 0.7 copy-start.6
  89.1 6.9 %collective-permute-start.12 = (f32[128,384]{1,0:T(8,128)}, f32[128,384]{1,0:T(8,128)S(1)}, u32[]{:S(2)}, u32[]{:S(2)}) collective-permute-start(f32[128,384]{1,0:T(8,128)} %meet.17), channel_id=1, source_target_pairs={{0,1},{1,0},{2,3},{3,2},{12,13},{13,12},{14,15},{15,14},{16,17},{1... | collective-permute-start | bytes 589832 | tf_op jit(solution)/shard_map/ppermute | solution.py:144
  96.0 140.0 %collective-permute-start.20 = (f32[2560,384]{1,0:T(8,128)}, f32[2560,384]{1,0:T(8,128)}, u32[]{:S(2)}, u32[]{:S(2)}) collective-permute-start(f32[2560,384]{1,0:T(8,128)} %get-tuple-element.29), channel_id=1, source_target_pairs={{4,0},{8,4},{12,8},{5,1},{9,5},{13,9},{6,2},{10,6},{14,10},{7,3},{... | collective-permute-start | bytes 11796488 | tf_op jit(solution)/shard_map/ppermute | solution.py:362
  99.2 10.8 %collective-permute-start.3 = (f32[1536,384]{1,0:T(8,128)}, f32[1536,384]{1,0:T(8,128)}, u32[]{:S(2)}, u32[]{:S(2)}) collective-permute-start(f32[1536,384]{1,0:T(8,128)} %get-tuple-element.21), channel_id=1, source_target_pairs={{4,0},{8,4},{12,8},{5,1},{9,5},{13,9},{6,2},{10,6},{14,10},{7,3},{... | collective-permute-start | bytes 7077896 | tf_op jit(solution)/shard_map/ppermute | solution.py:362
  101.9 150.2 %collective-permute-start.1 = (f32[3072,256]{1,0:T(8,128)}, f32[3072,256]{1,0:T(8,128)}, u32[]{:S(2)}, u32[]{:S(2)}) collective-permute-start(f32[3072,256]{1,0:T(8,128)} %get-tuple-element.19), channel_id=1, source_target_pairs={{0,12},{12,0},{1,13},{13,1},{2,14},{14,2},{3,15},{15,3},{16,28},{2... | collective-permute-start | bytes 9437192 | tf_op jit(solution)/shard_map/ppermute | solution.py:362
  103.8 13.7 %copy-start.1 = (f32[1536,384]{1,0:T(8,128)}, f32[1536,384]{1,0:T(8,128)S(1)}, u32[]{:S(2)}) copy-start(f32[1536,384]{1,0:T(8,128)S(1)} %collective-permute-done.2.left_ref) | copy-start | bytes 7077892
  103.8 156.3 %collective-permute-start = (f32[3072,256]{1,0:T(8,128)}, f32[3072,256]{1,0:T(8,128)}, u32[]{:S(2)}, u32[]{:S(2)}) collective-permute-start(f32[3072,256]{1,0:T(8,128)} %get-tuple-element.18), channel_id=1, source_target_pairs={{0,12},{12,0},{1,13},{13,1},{2,14},{14,2},{3,15},{15,3},{16,28},{2... | collective-permute-start | bytes 9437192 | tf_op jit(solution)/shard_map/ppermute | solution.py:362
  107.5 2.5 copy-start.3
  110.0 118.0 %collective-permute-start.16 = (f32[512,384]{1,0:T(8,128)}, f32[512,384]{1,0:T(8,128)S(1)}, u32[]{:S(2)}, u32[]{:S(2)}) collective-permute-start(f32[512,384]{1,0:T(8,128)} %get-tuple-element.25), channel_id=1, source_target_pairs={{0,4},{4,8},{8,12},{1,5},{5,9},{9,13},{2,6},{6,10},{10,14},{3,7},{... | collective-permute-start | bytes 2359304 | tf_op jit(solution)/shard_map/ppermute | solution.py:362
  118.2 125.2 %collective-permute-start.19 = (f32[512,384]{1,0:T(8,128)}, f32[512,384]{1,0:T(8,128)S(1)}, u32[]{:S(2)}, u32[]{:S(2)}) collective-permute-start(f32[512,384]{1,0:T(8,128)} %get-tuple-element.28), channel_id=1, source_target_pairs={{4,0},{8,4},{12,8},{5,1},{9,5},{13,9},{6,2},{10,6},{14,10},{7,3},{... | collective-permute-start | bytes 2359304 | tf_op jit(solution)/shard_map/ppermute | solution.py:362
  228.0 4.2 %copy-start.5 = (f32[512,384]{1,0:T(8,128)}, f32[512,384]{1,0:T(8,128)S(1)}, u32[]{:S(2)}) copy-start(f32[512,384]{1,0:T(8,128)S(1)} %collective-permute-done.16.left_ref) | copy-start | bytes 2359300
  228.0 47.9 %collective-permute-start.13 = (f32[128,384]{1,0:T(8,128)S(1)}, f32[128,384]{1,0:T(8,128)S(1)}, u32[]{:S(2)}, u32[]{:S(2)}) collective-permute-start(f32[128,384]{1,0:T(8,128)S(1)} %add.62), channel_id=1, source_target_pairs={{0,2},{1,3},{2,0},{3,1},{12,14},{13,15},{14,12},{15,13},{16,18},{1... | collective-permute-start | bytes 589832 | tf_op jit(solution)/shard_map/ppermute | solution.py:144
  236.0 16.0 %collective-permute-start.4 = (f32[8,128]{1,0:T(8,128)S(1)}, f32[8,128]{1,0:T(8,128)S(1)}, u32[]{:S(2)}, u32[]{:S(2)}) collective-permute-start(f32[8,128]{1,0:T(8,128)S(1)} %slice_add_fusion.1), channel_id=1, source_target_pairs={{0,4},{4,0},{8,12},{12,8},{1,5},{5,1},{9,13},{13,9},{2,6},{6,2},{1... | collective-permute-start | bytes 12296 | tf_op jit(solution)/shard_map/ppermute | solution.py:372
  243.4 4.0 %copy-start.2 = (f32[384,384]{1,0:T(8,128)S(1)}, f32[384,384]{1,0:T(8,128)}, u32[]{:S(2)}) copy-start(f32[384,384]{1,0:T(8,128)} %meet.21) | copy-start | bytes 1769476
  243.4 0.9 copy-start.4
  248.7 21.7 %collective-permute-start.22 = (f32[192,384]{1,0:T(8,128)S(1)}, f32[192,384]{1,0:T(8,128)S(1)}, u32[]{:S(2)}, u32[]{:S(2)}) collective-permute-start(f32[192,384]{1,0:T(8,128)S(1)} %get-tuple-element.31), channel_id=1, source_target_pairs={{0,3},{1,2},{2,1},{3,0},{4,7},{5,6},{6,5},{7,4},{8,11},{9,10},{10,... | collective-permute-start | bytes 884744 | tf_op jit(solution)/shard_map/ppermute | solution.py:144
  252.0 1.2 copy-start.7
  252.0 18.3 %collective-permute-start.24 = (f32[192,384]{1,0:T(8,128)S(1)}, f32[192,384]{1,0:T(8,128)}, u32[]{:S(2)}, u32[]{:S(2)}) collective-permute-start(f32[192,384]{1,0:T(8,128)S(1)} %get-tuple-element.32), channel_id=1, source_target_pairs={{0,1},{1,0},{2,3},{3,2},{4,5},{5,4},{6,7},{7,6},{8,9},{9,8},{10,11... | collective-permute-start | bytes 884744 | tf_op jit(solution)/shard_map/ppermute | solution.py:144
  252.1 21.4 %collective-permute-start.23 = (f32[192,384]{1,0:T(8,128)S(1)}, f32[192,384]{1,0:T(8,128)}, u32[]{:S(2)}, u32[]{:S(2)}) collective-permute-start(f32[192,384]{1,0:T(8,128)S(1)} %get-tuple-element.33), channel_id=1, source_target_pairs={{0,2},{1,3},{2,0},{3,1},{4,6},{5,7},{6,4},{7,5},{8,10},{9,11},{10,... | collective-permute-start | bytes 884744 | tf_op jit(solution)/shard_map/ppermute | solution.py:144
  267.0 22.4 %copy-start = (f32[256,384]{1,0:T(8,128)S(1)}, f32[256,384]{1,0:T(8,128)}, u32[]{:S(2)}) copy-start(f32[256,384]{1,0:T(8,128)} %meet.14.refs_0_) | copy-start | bytes 1179652
  267.0 22.4 %collective-permute-start.5 = (f32[256,384]{1,0:T(8,128)}, f32[256,384]{1,0:T(8,128)S(1)}, u32[]{:S(2)}, u32[]{:S(2)}) collective-permute-start(f32[256,384]{1,0:T(8,128)} %meet.14.refs_0_), channel_id=1, source_target_pairs={{0,1},{1,0},{2,3},{3,2},{12,13},{13,12},{14,15},{15,14},{16,17},{1... | collective-permute-start | bytes 1179656 | tf_op jit(solution)/shard_map/ppermute | solution.py:144
  274.5 16.9 %collective-permute-start.25 = (f32[96,384]{1,0:T(8,128)S(1)}, f32[96,384]{1,0:T(8,128)S(1)}, u32[]{:S(2)}, u32[]{:S(2)}) collective-permute-start(f32[96,384]{1,0:T(8,128)S(1)} %slice.19), channel_id=1, source_target_pairs={{0,4},{4,8},{8,12},{1,5},{5,9},{9,13},{2,6},{6,10},{10,14},{3,7},{... | collective-permute-start | bytes 442376 | tf_op jit(solution)/shard_map/ppermute | solution.py:390
  275.9 19.3 %collective-permute-start.14 = (f32[128,384]{1,0:T(8,128)S(1)}, f32[128,384]{1,0:T(8,128)S(1)}, u32[]{:S(2)}, u32[]{:S(2)}) collective-permute-start(f32[128,384]{1,0:T(8,128)S(1)} %add.63), channel_id=1, source_target_pairs={{0,8},{12,4},{1,9},{13,5},{2,10},{14,6},{3,11},{15,7},{16,24},{28,... | collective-permute-start | bytes 589832 | tf_op jit(solution)/shard_map/ppermute | solution.py:191
  289.5 21.4 %collective-permute-start.6 = (f32[256,384]{1,0:T(8,128)S(1)}, f32[256,384]{1,0:T(8,128)S(1)}, u32[]{:S(2)}, u32[]{:S(2)}) collective-permute-start(f32[256,384]{1,0:T(8,128)S(1)} %add.60), channel_id=1, source_target_pairs={{0,2},{1,3},{2,0},{3,1},{12,14},{13,15},{14,12},{15,13},{16,18},{1... | collective-permute-start | bytes 1179656 | tf_op jit(solution)/shard_map/ppermute | solution.py:144
  291.5 20.8 %collective-permute-start.28 = (f32[96,384]{1,0:T(8,128)S(1)}, f32[96,384]{1,0:T(8,128)S(1)}, u32[]{:S(2)}, u32[]{:S(2)}) collective-permute-start(f32[96,384]{1,0:T(8,128)S(1)} %slice_add_fusion), channel_id=1, source_target_pairs={{0,3},{1,2},{2,1},{3,0},{4,7},{5,6},{6,5},{7,4},{8,11},{9,10},{10,... | collective-permute-start | bytes 442376 | tf_op jit(solution)/shard_map/ppermute | solution.py:144
  293.8 20.3 %collective-permute-start.27 = (f32[96,384]{1,0:T(8,128)S(1)}, f32[96,384]{1,0:T(8,128)S(1)}, u32[]{:S(2)}, u32[]{:S(2)}) collective-permute-start(f32[96,384]{1,0:T(8,128)S(1)} %slice_add_fusion), channel_id=1, source_target_pairs={{0,2},{1,3},{2,0},{3,1},{4,6},{5,7},{6,4},{7,5},{8,10},{9,11},{10,... | collective-permute-start | bytes 442376 | tf_op jit(solution)/shard_map/ppermute | solution.py:144
  295.2 18.9 %collective-permute-start.26 = (f32[96,384]{1,0:T(8,128)S(1)}, f32[96,384]{1,0:T(8,128)S(1)}, u32[]{:S(2)}, u32[]{:S(2)}) collective-permute-start(f32[96,384]{1,0:T(8,128)S(1)} %slice_add_fusion), channel_id=1, source_target_pairs={{0,1},{1,0},{2,3},{3,2},{4,5},{5,4},{6,7},{7,6},{8,9},{9,8},{10,11... | collective-permute-start | bytes 442376 | tf_op jit(solution)/shard_map/ppermute | solution.py:144
  295.2 29.2 %collective-permute-start.15 = (f32[128,384]{1,0:T(8,128)S(1)}, f32[128,384]{1,0:T(8,128)S(1)}, u32[]{:S(2)}, u32[]{:S(2)}) collective-permute-start(f32[128,384]{1,0:T(8,128)S(1)} %broadcast_select_fusion.3), channel_id=1, source_target_pairs={{0,4},{4,0},{8,12},{12,8},{1,5},{5,1},{9,13},{13,9},{2,6},{6,2},{1... | collective-permute-start | bytes 589832 | tf_op jit(solution)/shard_map/ppermute | solution.py:193
  310.9 11.7 %collective-permute-start.7 = (f32[256,384]{1,0:T(8,128)S(1)}, f32[256,384]{1,0:T(8,128)S(1)}, u32[]{:S(2)}, u32[]{:S(2)}) collective-permute-start(f32[256,384]{1,0:T(8,128)S(1)} %add.61), channel_id=1, source_target_pairs={{0,8},{12,4},{1,9},{13,5},{2,10},{14,6},{3,11},{15,7},{16,24},{28,... | collective-permute-start | bytes 1179656 | tf_op jit(solution)/shard_map/ppermute | solution.py:191
  322.0 0.8 collective-permute-start.29
  322.7 7.6 %collective-permute-start.8 = (f32[256,384]{1,0:T(8,128)S(1)}, f32[256,384]{1,0:T(8,128)S(1)}, u32[]{:S(2)}, u32[]{:S(2)}) collective-permute-start(f32[256,384]{1,0:T(8,128)S(1)} %broadcast_select_fusion), channel_id=1, source_target_pairs={{0,4},{4,0},{8,12},{12,8},{1,5},{5,1},{9,13},{13,9},{2,6},{6,2},{1... | collective-permute-start | bytes 1179656 | tf_op jit(solution)/shard_map/ppermute | solution.py:193
  323.2 3.3 collective-permute-start.30
  326.8 7.2 %collective-permute-start.33 = (f32[96,384]{1,0:T(8,128)S(1)}, f32[96,384]{1,0:T(8,128)S(1)}, u32[]{:S(2)}, u32[]{:S(2)}) collective-permute-start(f32[96,384]{1,0:T(8,128)S(1)} %convolution_select_fusion), channel_id=1, source_target_pairs={{0,3},{1,2},{2,1},{3,0},{4,7},{5,6},{6,5},{7,4},{8,11},{9,10},{10,... | collective-permute-start | bytes 442376 | tf_op jit(solution)/shard_map/ppermute | solution.py:144
  327.9 13.0 %collective-permute-start.32 = (f32[96,384]{1,0:T(8,128)S(1)}, f32[96,384]{1,0:T(8,128)S(1)}, u32[]{:S(2)}, u32[]{:S(2)}) collective-permute-start(f32[96,384]{1,0:T(8,128)S(1)} %convolution_select_fusion), channel_id=1, source_target_pairs={{0,2},{1,3},{2,0},{3,1},{4,6},{5,7},{6,4},{7,5},{8,10},{9,11},{10,... | collective-permute-start | bytes 442376 | tf_op jit(solution)/shard_map/ppermute | solution.py:144
  327.9 13.0 %collective-permute-start.31 = (f32[96,384]{1,0:T(8,128)S(1)}, f32[96,384]{1,0:T(8,128)S(1)}, u32[]{:S(2)}, u32[]{:S(2)}) collective-permute-start(f32[96,384]{1,0:T(8,128)S(1)} %convolution_select_fusion), channel_id=1, source_target_pairs={{0,1},{1,0},{2,3},{3,2},{4,5},{5,4},{6,7},{7,6},{8,9},{9,8},{10,11... | collective-permute-start | bytes 442376 | tf_op jit(solution)/shard_map/ppermute | solution.py:144
